TPU v7x, 128 devices: a whole 4x4x4 slice. The times are simulated.
128 devices in a mesh: row: 8 (over z, x_hi), col: 16 (over x_lo, y, core).
Axes of the slice: x: 4 (x_hi: 2, x_lo: 2; x = x_hi * 2 + x_lo), y: 4, z: 4, core: 2. Of those that a mesh axis runs over, the one named last changes fastest.
Arguments:
- ingest_features: bfloat16 [32768, 1536], P(('row', 'col')), may hold values from -40 to 40
- node_map: int32 [32768], P(('row', 'col')), may hold values from 0 to 16383, as said below
- unit_rows: int32 [128], P(('row', 'col')), may hold values from 0 to 256, as said below
- tile_ids: int32 [12288, 2], P(('row', 'col')), may hold values from 0 to 128, as said below
- tile_values: bfloat16 [12288, 128, 128], P(('row', 'col')), may hold values from -40 to 40
- mix_in: bfloat16 [128, 128], replicated, may hold values from -0.5 to 0.5
- mix_out: bfloat16 [128, 128], replicated, may hold values from -0.5 to 0.5
Outputs:
- residual: float32 [16384, 1536], P(('row', 'col'))
Inputs may be any that keep to these rules, and one draw needn't show every extreme that they name: `node_map`: for every unit u the first unit_rows[u] of its 256 slots name distinct nodes, and all units' such slots together name every node exactly once; at most 2 of them of one unit name nodes of one partition (nodes k * 128 to (k + 1) * 128 - 1), and one unit names exactly 2 in every partition. Entries of the other slots are arbitrary nodes. `unit_rows`: one unit delivers 256 rows. `tile_ids`: slots k * 96 to (k + 1) * 96 - 1 hold first some distinct tiles whose row tile lies in row block k // 16 (tile rows (16 times that) onward) and whose column tile lies in column block k % 16, then padding slots whose row tile and column tile are both 16384 // 128. Some blocks have no padding slot.
All inputs are finite; a program needn't handle non-finite values.
Results may differ from a plain program's by a relative error of at most 0.0095.
Values may be sent and summed in bfloat16 or wider, within the bound.
A program may use at most 64 MiB of HBM per device.

v0:
```python
import jax
import jax.numpy as jnp
from jax import lax
from jax.sharding import PartitionSpec as P

CH = 128
TILE = 128
PIECE = 128
epsilon = 1e-05


def normalize(values):
    groups = values.reshape(-1, CH)
    power = jnp.mean(groups * groups, axis=-1, keepdims=True)
    return (groups * lax.rsqrt(power + epsilon)).astype(jnp.bfloat16)


def encode(totals, mix_in):
    row_total = totals.shape[0]
    mixed = jnp.dot(normalize(totals), mix_in, preferred_element_type=jnp.float32)
    return jax.nn.gelu(mixed, approximate=False).astype(jnp.bfloat16).reshape(row_total, -1)


def dense_block(tile_ids, tile_values, row_index, col_index, row_tiles, col_tiles):
    local_rows = tile_ids[:, 0] - row_index * row_tiles
    local_cols = tile_ids[:, 1] - col_index * col_tiles
    tile_edge = tile_values.shape[1]
    tile_grid = jnp.zeros((row_tiles, col_tiles, tile_edge, tile_edge), tile_values.dtype)
    tile_grid = tile_grid.at[local_rows, local_cols].set(tile_values, mode="drop")
    return tile_grid.transpose(0, 2, 1, 3).reshape(row_tiles * tile_edge, col_tiles * tile_edge)


def local(ingest_features, node_map, unit_rows, tile_ids, tile_values, mix_in, mix_out):
    row_count = lax.axis_size("row")
    col_count = lax.axis_size("col")
    unit_count = row_count * col_count
    slots_held = node_map.shape[0]
    per_pair = slots_held // unit_count
    feature_width = ingest_features.shape[1]
    owner = node_map // PIECE
    live = jnp.arange(slots_held, dtype=jnp.int32) < unit_rows[0]
    member = (
        (owner[:, None] == jnp.arange(unit_count, dtype=jnp.int32)[None, :]) & live[:, None]
    ).astype(jnp.int32)
    earlier = jnp.cumsum(member, axis=0) - member
    rank_within = jnp.sum(earlier * member, axis=1)
    target = jnp.where(live, owner * per_pair + rank_within, unit_count * per_pair)
    outgoing = (
        jnp.zeros((unit_count * per_pair, feature_width), jnp.bfloat16)
        .at[target]
        .set(ingest_features, mode="drop")
    )
    placing = (
        jnp.full((unit_count * per_pair,), -1, jnp.int32)
        .at[target]
        .set(node_map % PIECE, mode="drop")
    )
    arrived, arrived_at = (
        lax.all_to_all(
            outgoing.reshape(unit_count, per_pair, feature_width),
            ("row", "col"),
            split_axis=0,
            concat_axis=0,
            tiled=True,
        ),
        lax.all_to_all(
            placing.reshape(unit_count, per_pair),
            ("row", "col"),
            split_axis=0,
            concat_axis=0,
            tiled=True,
        ),
    )
    arrived = arrived.reshape(-1, feature_width)
    arrived_at = arrived_at.reshape(-1)
    landing = jnp.where(arrived_at >= 0, arrived_at, PIECE)
    features = jnp.zeros((PIECE, feature_width), jnp.bfloat16).at[landing].set(arrived, mode="drop")
    row_tiles = col_count * PIECE // TILE
    col_tiles = row_count * PIECE // TILE
    block = dense_block(
        tile_ids, tile_values, lax.axis_index("row"), lax.axis_index("col"), row_tiles, col_tiles
    )
    strip = block
    back_part = lax.dot_general(
        strip,
        lax.all_gather(features, "col", axis=0, tiled=True),
        (((0,), (0,)), ((), ())),
        preferred_element_type=jnp.float32,
    )
    back_own = lax.psum_scatter(
        back_part.astype(jnp.bfloat16), "row", scatter_dimension=0, tiled=True
    ).astype(jnp.float32)
    hidden = lax.all_gather(encode(back_own, mix_in), "row", axis=0, tiled=True)
    strip = block
    forward_sum = lax.psum_scatter(
        jnp.dot(strip, hidden, preferred_element_type=jnp.float32).astype(jnp.bfloat16),
        "col",
        scatter_dimension=0,
        tiled=True,
    ).astype(jnp.float32)
    recon = jnp.dot(normalize(forward_sum), mix_out, preferred_element_type=jnp.float32).reshape(
        PIECE, feature_width
    )
    return features.astype(jnp.float32) - recon


def solution(mesh):
    return jax.shard_map(
        local,
        mesh=mesh,
        in_specs=(
            P(("row", "col"), None),
            P(("row", "col")),
            P(("row", "col")),
            P(("row", "col"), None),
            P(("row", "col"), None, None),
            P(),
            P(),
        ),
        out_specs=P(("row", "col"), None),
        check_vma=False,
    )
```

profile of v0, /device:TPU:0, one launch (start us, length us, event | category | flops | bytes accessed | tf_op | source)
XLA Modules:
  0.0 343.9 jit_solution(6542489902503923748)
XLA Ops:
  6.5 0.0 copy-start
  6.5 0.0 copy-start.4
  7.2 0.7 and_select_fusion
  7.9 0.1 copy.11
  8.1 0.3 fusion.26
  8.5 0.2 fusion.28
  8.7 1.4 scatter_custom_fusion
  10.1 0.8 all_to_all.9
  10.9 11.1 %all-to-all-start = ((s32[128,1,2]{2,1,0:T(1,128)}), s32[128,1,2]{2,1,0:T(1,128)S(1)}, u32[]{:S(2)}, u32[]{:S(2)}) async-start(s32[128,1,2]{2,1,0:T(1,128)} %bitcast.5), calls=%async_computation | async-start | bytes 131072 | tf_op jit(solution)/shard_map/all_to_all | solution.py:66
  22.0 2.6 scatter_custom_fusion.1
  24.6 1.2 reshape.107
  25.8 5.5 %all-to-all-done = s32[128,1,2]{2,1,0:T(1,128)S(1)} async-done(((s32[128,1,2]{2,1,0:T(1,128)}), s32[128,1,2]{2,1,0:T(1,128)S(1)}, u32[]{:S(2)}, u32[]{:S(2)}) %all-to-all-start) | async-done | bytes 1056 | tf_op jit(solution)/shard_map/all_to_all | solution.py:66
  31.3 4.7 %all-to-all-start.1 = ((bf16[128,2,1536]{2,1,0:T(2,128)(2,1)}), bf16[128,2,1536]{2,1,0:T(2,128)(2,1)S(1)}, u32[]{:S(2)}, u32[]{:S(2)}) async-start(bf16[128,2,1536]{2,1,0:T(2,128)(2,1)} %reshape.107), calls=%async_computation.1 | async-start | bytes 1572864 | tf_op jit(solution)/shard_map/all_to_all | solution.py:59
  36.0 0.0 all-gather.3.cloned.1.call-start
  36.1 0.6 broadcast.166
  36.7 0.8 reduce.3
  37.5 0.1 reshape.106
  37.7 14.6 %all-to-all-done.1 = bf16[128,2,1536]{2,1,0:T(2,128)(2,1)S(1)} async-done(((bf16[128,2,1536]{2,1,0:T(2,128)(2,1)}), bf16[128,2,1536]{2,1,0:T(2,128)(2,1)S(1)}, u32[]{:S(2)}, u32[]{:S(2)}) %all-to-all-start.1) | async-done | bytes 786464 | tf_op jit(solution)/shard_map/all_to_all | solution.py:59
  52.3 1.2 reshape.140
  53.5 0.0 copy-start.2
  53.5 3.2 scatter_custom_fusion.2
  56.7 0.0 all-gather.3.cloned.1.call-update
  56.8 0.2 reduce-scatter.3.cloned.1.call-start
  57.0 0.0 copy-done.4
  57.0 3.1 broadcast_in_dim.34
  60.2 0.0 copy-done.2
  60.2 13.7 %scatter_fusion = bf16[16,8,128,128]{3,2,1,0:T(8,128)(2,1)} fusion(bf16[16,8,128,128]{3,2,1,0:T(8,128)(2,1)} %broadcast_in_dim.34, s32[96]{0:T(128)S(1)} %fusion.36, bf16[96,128,128]{2,1,0:T(8,128)(2,1)S(1)} %copy-done.2), kind=kCustom, calls=%fused_computation.3 | custom fusion | bytes 9437952 | tf_op jit(solution)/shard_map/scatter | solution.py:29
  73.9 7.8 %copy.14 = bf16[16,128,8,128]{3,2,1,0:T(8,128)(2,1)} copy(bf16[16,128,8,128]{3,1,2,0:T(8,128)(2,1)} %bitcast.40) | data formatting | bytes 8388608 | tf_op jit(solution)/shard_map/transpose | solution.py:30
  81.7 13.3 %all-gather.3.cloned.1.call-done = bf16[2048,1536]{1,0:T(8,128)(2,1)} async-done(((bf16[128,1536]{1,0:T(8,128)(2,1)}), bf16[2048,1536]{1,0:T(8,128)(2,1)}) %all-gather.3.cloned.1.call-update) | async-done | bytes 6291472 | tf_op jit(solution)/shard_map/all_gather | solution.py:86
  95.0 11.4 %fusion.3 = bf16[1024,1536]{1,0:T(8,128)(2,1)} fusion(bf16[2048,1536]{1,0:T(8,128)(2,1)} %all-gather.3.cloned.1.call-done, bf16[256,8,8,128]{3,2,1,0:T(8,128)(2,1)} %bitcast.41), kind=kOutput, calls=%fused_computation.8 | convolution fusion | flops 6444023808 | bytes 13631488 | tf_op jit(solution)/shard_map/dot_general | solution.py:84
  106.4 0.0 reduce-scatter.3.cloned.1.call-update
  106.5 0.0 all-gather.5.cloned.1.call-start
  106.5 80.5 %reduce-scatter.3.cloned.1.call-done = bf16[128,1536]{1,0:T(8,128)(2,1)} async-done(((bf16[1024,1536]{1,0:T(8,128)(2,1)}), bf16[128,1536]{1,0:T(8,128)(2,1)}) %reduce-scatter.3.cloned.1.call-update) | async-done | bytes 393232 | tf_op jit(solution)/shard_map/reduce_scatter | solution.py:90
  187.0 1.4 reshape.117
  188.4 0.3 multiply_reduce_fusion.1
  188.7 0.0 copy-done
  188.7 2.4 fusion.10
  191.1 1.2 reshape.112
  192.3 0.0 all-gather.5.cloned.1.call-update
  192.3 0.3 reduce-scatter.5.cloned.1.call-start
  192.6 61.5 %all-gather.5.cloned.1.call-done = bf16[1024,1536]{1,0:T(8,128)(2,1)} async-done(((bf16[128,1536]{1,0:T(8,128)(2,1)}), bf16[1024,1536]{1,0:T(8,128)(2,1)}) %all-gather.5.cloned.1.call-update) | async-done | bytes 3145744 | tf_op jit(solution)/shard_map/all_gather | solution.py:93
  254.1 11.3 %convolution_convert_fusion = bf16[2048,1536]{1,0:T(8,128)(2,1)} fusion(bf16[1024,1536]{1,0:T(8,128)(2,1)} %all-gather.5.cloned.1.call-done, bf16[256,8,8,128]{3,2,1,0:T(8,128)(2,1)} %bitcast.42), kind=kOutput, calls=%fused_computation.4 | convolution fusion | flops 6445596672 | bytes 13631488 | tf_op jit(solution)/shard_map/dot_general | solution.py:96
  265.4 0.0 copy-start.3
  265.4 0.0 copy-start.1
  265.4 0.0 reduce-scatter.5.cloned.1.call-update
  265.5 68.6 %reduce-scatter.5.cloned.1.call-done = bf16[128,1536]{1,0:T(8,128)(2,1)} async-done(((bf16[2048,1536]{1,0:T(8,128)(2,1)}), bf16[128,1536]{1,0:T(8,128)(2,1)}) %reduce-scatter.5.cloned.1.call-update) | async-done | bytes 393232 | tf_op jit(solution)/shard_map/reduce_scatter | solution.py:95
  334.1 1.4 reshape.119
  335.5 0.3 multiply_reduce_fusion
  335.8 0.0 copy-done.3
  335.8 0.4 fusion.19
  336.2 0.1 reshape.115
  336.4 0.0 copy-done.1
  336.4 1.0 convert_subtract_fusion
  (13 shorter events, 0.1 us)
Async XLA Ops:
  6.5 182.2 %copy-start = (bf16[128,128]{1,0:T(8,128)(2,1)S(1)}, bf16[128,128]{1,0:T(8,128)(2,1)}, u32[]{:S(2)}) copy-start(bf16[128,128]{1,0:T(8,128)(2,1)} %param.12) | copy-start | bytes 98308
  6.5 50.5 %copy-start.4 = (s32[96,2]{0,1:T(2,128)S(1)}, s32[96,2]{0,1:T(2,128)}, u32[]{:S(2)}) copy-start(s32[96,2]{0,1:T(2,128)} %param.10) | copy-start | bytes 2308
  10.9 20.5 %all-to-all-start = ((s32[128,1,2]{2,1,0:T(1,128)}), s32[128,1,2]{2,1,0:T(1,128)S(1)}, u32[]{:S(2)}, u32[]{:S(2)}) async-start(s32[128,1,2]{2,1,0:T(1,128)} %bitcast.5), calls=%async_computation | async-start | bytes 131072 | tf_op jit(solution)/shard_map/all_to_all | solution.py:66
  31.3 21.0 %all-to-all-start.1 = ((bf16[128,2,1536]{2,1,0:T(2,128)(2,1)}), bf16[128,2,1536]{2,1,0:T(2,128)(2,1)S(1)}, u32[]{:S(2)}, u32[]{:S(2)}) async-start(bf16[128,2,1536]{2,1,0:T(2,128)(2,1)} %reshape.107), calls=%async_computation.1 | async-start | bytes 1572864 | tf_op jit(solution)/shard_map/all_to_all | solution.py:59
  36.0 59.0 %all-gather.3.cloned.1.call-start = ((), (), s32[]{:S(2)}) async-start(), calls=%async_computation.4 | async-start | bytes 6684672 | tf_op jit(solution)/shard_map/all_gather | solution.py:86
  53.5 6.7 %copy-start.2 = (bf16[96,128,128]{2,1,0:T(8,128)(2,1)S(1)}, bf16[96,128,128]{2,1,0:T(8,128)(2,1)}, u32[]{:S(2)}) copy-start(bf16[96,128,128]{2,1,0:T(8,128)(2,1)} %param.11) | copy-start | bytes 9437188
  56.8 130.2 %reduce-scatter.3.cloned.1.call-start = ((), (), s32[]{:S(2)}) async-start(), calls=%async_computation.5 | async-start | bytes 3538944 | tf_op jit(solution)/shard_map/reduce_scatter | solution.py:90
  106.5 147.7 %all-gather.5.cloned.1.call-start = ((), (), s32[]{:S(2)}) async-start(), calls=%async_computation.6 | async-start | bytes 3538944 | tf_op jit(solution)/shard_map/all_gather | solution.py:93
  192.3 141.7 %reduce-scatter.5.cloned.1.call-start = ((), (), s32[]{:S(2)}) async-start(), calls=%async_computation.7 | async-start | bytes 6684672 | tf_op jit(solution)/shard_map/reduce_scatter | solution.py:95
  265.4 70.4 %copy-start.3 = (bf16[128,128]{1,0:T(8,128)(2,1)S(1)}, bf16[128,128]{1,0:T(8,128)(2,1)}, u32[]{:S(2)}) copy-start(bf16[128,128]{1,0:T(8,128)(2,1)} %param.13) | copy-start | bytes 98308
  265.4 70.9 %copy-start.1 = (bf16[128,1536]{1,0:T(8,128)(2,1)S(1)}, bf16[128,1536]{1,0:T(8,128)(2,1)}, u32[]{:S(2)}) copy-start(bf16[128,1536]{1,0:T(8,128)(2,1)} %scatter_custom_fusion.2) | copy-start | bytes 1179652
Sparse Core Ops, SparseCore 0:
  56.9 38.0 all-gather.2
  106.6 80.3 reduce-scatter.2
  192.5 61.6 all-gather.4
  265.6 68.4 reduce-scatter.4
where the time goes:
time: 345 us; the launch traced here: 344 us
  waiting for transfers between devices  244 us (71%)
  local copies, waits for them, and re-layouts  40.1 us (12%)
  matrix products  25.5 us (7%)
  starting transfers between devices  16.4 us (5%)
  between operations  14 us (4%)
  other arithmetic  3.71 us (1%)
    reduce_scatter x1, waiting for transfers between devices, local(): lax.psum_scatter(back_part.astype(jnp.bfloat16), 'row', scatter_dimension...  80.5 us
    reduce_scatter x1, waiting for transfers between devices, local(): lax.psum_scatter(jnp.dot(strip, hidden, preferred_element_type=jnp.float3...  68.6 us
    all_gather x1, waiting for transfers between devices, local(): hidden = lax.all_gather(encode(back_own, mix_in), 'row', axis=0, tiled=True)  61.5 us
    all_to_all x1, waiting for transfers between devices, local(): lax.all_to_all(outgoing.reshape(unit_count, per_pair, feature_width), ('r...  14.6 us
    scatter x1, local copies, waits for them, and re-layouts, dense_block(): tile_grid.at[local_rows, local_cols].set(tile_values, mode='drop')  13.7 us
    all_gather x1, waiting for transfers between devices, local(): lax.all_gather(features, 'col', axis=0, tiled=True)  13.3 us
    dot_general x1, matrix products, local(): lax.dot_general(strip, lax.all_gather(features, 'col', axis=0, tiled=True...  11.4 us
    dot_general x1, matrix products, local(): jnp.dot(strip, hidden, preferred_element_type=jnp.float32)  11.3 us
  transfers between devices with their start and end apart: 6, of which 6 were waited for; matrix products, arithmetic and copies ran while one was open for 9% of the time, Pallas kernels for 0%

commit v1 on v0

--- a/solution.py
+++ b/solution.py
@@ -83,7 +83,10 @@
     strip = block
     back_part = lax.dot_general(
         strip,
-        lax.all_gather(features, "col", axis=0, tiled=True),
+        jnp.concatenate(
+            jax.lax.all_to_all(jnp.stack(jax.lax.axis_size("col") * [features]), "col", 0, 0),
+            axis=0,
+        ),
         (((0,), (0,)), ((), ())),
         preferred_element_type=jnp.float32,
     )

time: 345 us -> 403 us (1.17)
  waiting for transfers between devices: 244 us -> 295 us
  starting transfers between devices: 16.4 us -> 21.1 us
    all_to_all x0 -> x1, waiting for transfers between devices: none -> 61.3 us  [local(): jax.lax.all_to_all(jnp.stack(jax.lax.axis_size('col') * [features]), 'col...]
    all_gather x1 -> x0, waiting for transfers between devices: 13.3 us -> none  [local(): lax.all_gather(features, 'col', axis=0, tiled=True)]
    all_to_all x0 -> x1, starting transfers between devices: none -> 4.76 us  [local(): jax.lax.all_to_all(jnp.stack(jax.lax.axis_size('col') * [features]), 'col...]
  transfers between devices with their start and end apart: 6 -> 6, of which waited for: 6 -> 6; matrix products, arithmetic and copies ran while one was open for 9% -> 8% of each run, Pallas kernels for 0% -> 0%
where the time goes in v1:
time: 403 us; the launch traced here: 402 us
  waiting for transfers between devices  295 us (73%)
  local copies, waits for them, and re-layouts  42.8 us (11%)
  matrix products  25.6 us (6%)
  starting transfers between devices  21.1 us (5%)
  between operations  14 us (3%)
    reduce_scatter x1, waiting for transfers between devices, local(): lax.psum_scatter(back_part.astype(jnp.bfloat16), 'row', scatter_dimension...  83.2 us
    reduce_scatter x1, waiting for transfers between devices, local(): lax.psum_scatter(jnp.dot(strip, hidden, preferred_element_type=jnp.float3...  68.6 us
    all_gather x1, waiting for transfers between devices, local(): hidden = lax.all_gather(encode(back_own, mix_in), 'row', axis=0, tiled=True)  61.5 us
    all_to_all x1, waiting for transfers between devices, local(): jax.lax.all_to_all(jnp.stack(jax.lax.axis_size('col') * [features]), 'col...  61.3 us
    scatter x1, local copies, waits for them, and re-layouts, dense_block(): tile_grid.at[local_rows, local_cols].set(tile_values, mode='drop')  15.7 us
    all_to_all x1, waiting for transfers between devices, local(): lax.all_to_all(outgoing.reshape(unit_count, per_pair, feature_width), ('r...  14.7 us
    dot_general x1, matrix products, local(): lax.dot_general(strip, jnp.concatenate(jax.lax.all_to_all(jnp.stack(jax.l...  11.5 us
    dot_general x1, matrix products, local(): jnp.dot(strip, hidden, preferred_element_type=jnp.float32)  11.3 us
  transfers between devices with their start and end apart: 6, of which 6 were waited for; matrix products, arithmetic and copies ran while one was open for 8% of the time, Pallas kernels for 0%

profile of v1, /device:TPU:0, one launch (start us, length us, event | category | flops | bytes accessed | tf_op | source)
XLA Modules:
  0.0 402.1 jit_solution(14900453024285488252)
XLA Ops:
  6.5 0.0 copy-start
  6.5 0.7 and_select_fusion
  7.2 0.1 copy.11
  8.0 0.3 fusion.26
  8.5 0.2 fusion.28
  8.7 1.4 scatter_custom_fusion
  10.1 0.8 all_to_all.12
  10.9 11.1 %all-to-all-start = ((s32[128,1,2]{2,1,0:T(1,128)}), s32[128,1,2]{2,1,0:T(1,128)S(1)}, u32[]{:S(2)}, u32[]{:S(2)}) async-start(s32[128,1,2]{2,1,0:T(1,128)} %bitcast.5), calls=%async_computation | async-start | bytes 131072 | tf_op jit(solution)/shard_map/all_to_all | solution.py:66
  22.0 2.6 scatter_custom_fusion.1
  24.6 1.2 reshape.112
  25.8 5.5 %all-to-all-done = s32[128,1,2]{2,1,0:T(1,128)S(1)} async-done(((s32[128,1,2]{2,1,0:T(1,128)}), s32[128,1,2]{2,1,0:T(1,128)S(1)}, u32[]{:S(2)}, u32[]{:S(2)}) %all-to-all-start) | async-done | bytes 1056 | tf_op jit(solution)/shard_map/all_to_all | solution.py:66
  31.3 4.7 %all-to-all-start.1 = ((bf16[128,2,1536]{2,1,0:T(2,128)(2,1)}), bf16[128,2,1536]{2,1,0:T(2,128)(2,1)S(1)}, u32[]{:S(2)}, u32[]{:S(2)}) async-start(bf16[128,2,1536]{2,1,0:T(2,128)(2,1)} %reshape.112), calls=%async_computation.1 | async-start | bytes 1572864 | tf_op jit(solution)/shard_map/all_to_all | solution.py:59
  36.0 0.6 broadcast.168
  36.6 0.8 reduce.3
  37.5 0.1 reshape.111
  37.6 14.7 %all-to-all-done.1 = bf16[128,2,1536]{2,1,0:T(2,128)(2,1)S(1)} async-done(((bf16[128,2,1536]{2,1,0:T(2,128)(2,1)}), bf16[128,2,1536]{2,1,0:T(2,128)(2,1)S(1)}, u32[]{:S(2)}, u32[]{:S(2)}) %all-to-all-start.1) | async-done | bytes 786464 | tf_op jit(solution)/shard_map/all_to_all | solution.py:59
  52.3 0.3 reshape.146
  52.6 1.9 scatter_custom_fusion.2
  54.5 3.3 stack.2
  57.7 0.0 copy-start.2
  57.7 4.8 %all-to-all-start.2 = ((bf16[16,128,1536]{2,1,0:T(8,128)(2,1)}), bf16[16,128,1536]{2,1,0:T(8,128)(2,1)}, u32[]{:S(2)}, u32[]{:S(2)}) async-start(bf16[16,128,1536]{2,1,0:T(8,128)(2,1)} %stack.2), calls=%async_computation.2 | async-start | bytes 12582912 | tf_op jit(solution)/shard_map/all_to_all | solution.py:87
  62.5 0.2 reduce-scatter.3.cloned.1.call-start
  62.7 0.0 copy-done.2
  62.8 3.0 broadcast_in_dim.34
  65.7 15.7 %scatter_fusion = bf16[16,8,128,128]{3,2,1,0:T(8,128)(2,1)} fusion(bf16[16,8,128,128]{3,2,1,0:T(8,128)(2,1)} %broadcast_in_dim.34, s32[96]{0:T(128)S(1)} %fusion.36, bf16[96,128,128]{2,1,0:T(8,128)(2,1)} %param.11), kind=kCustom, calls=%fused_computation.3 | custom fusion | bytes 9437952 | tf_op jit(solution)/shard_map/scatter | solution.py:29
  81.4 7.7 %copy.14 = bf16[16,128,8,128]{3,2,1,0:T(8,128)(2,1)} copy(bf16[16,128,8,128]{3,1,2,0:T(8,128)(2,1)} %bitcast.37) | data formatting | bytes 8388608 | tf_op jit(solution)/shard_map/transpose | solution.py:30
  89.1 61.3 %all-to-all-done.2 = bf16[16,128,1536]{2,1,0:T(8,128)(2,1)} async-done(((bf16[16,128,1536]{2,1,0:T(8,128)(2,1)}), bf16[16,128,1536]{2,1,0:T(8,128)(2,1)}, u32[]{:S(2)}, u32[]{:S(2)}) %all-to-all-start.2) | async-done | bytes 6291488 | tf_op jit(solution)/shard_map/all_to_all | solution.py:87
  150.5 11.5 %fusion.3 = bf16[1024,1536]{1,0:T(8,128)(2,1)} fusion(bf16[2048,1536]{1,0:T(8,128)(2,1)} %bitcast.9, bf16[256,8,8,128]{3,2,1,0:T(8,128)(2,1)} %bitcast.38), kind=kOutput, calls=%fused_computation.8 | convolution fusion | flops 6444023808 | bytes 13631488 | tf_op jit(solution)/shard_map/dot_general | solution.py:84
  162.0 0.0 reduce-scatter.3.cloned.1.call-update
  162.0 0.0 all-gather.2.cloned.1.call-start
  162.0 83.2 %reduce-scatter.3.cloned.1.call-done = bf16[128,1536]{1,0:T(8,128)(2,1)} async-done(((bf16[1024,1536]{1,0:T(8,128)(2,1)}), bf16[128,1536]{1,0:T(8,128)(2,1)}) %reduce-scatter.3.cloned.1.call-update) | async-done | bytes 393232 | tf_op jit(solution)/shard_map/reduce_scatter | solution.py:93
  245.2 1.4 reshape.123
  246.7 0.3 multiply_reduce_fusion.1
  246.9 0.0 copy-done
  247.0 2.4 fusion.10
  249.4 1.2 reshape.118
  250.6 0.0 all-gather.2.cloned.1.call-update
  250.6 0.3 reduce-scatter.5.cloned.1.call-start
  250.9 61.5 %all-gather.2.cloned.1.call-done = bf16[1024,1536]{1,0:T(8,128)(2,1)} async-done(((bf16[128,1536]{1,0:T(8,128)(2,1)}), bf16[1024,1536]{1,0:T(8,128)(2,1)}) %all-gather.2.cloned.1.call-update) | async-done | bytes 3145744 | tf_op jit(solution)/shard_map/all_gather | solution.py:96
  312.4 11.3 %convolution_convert_fusion = bf16[2048,1536]{1,0:T(8,128)(2,1)} fusion(bf16[1024,1536]{1,0:T(8,128)(2,1)} %all-gather.2.cloned.1.call-done, bf16[256,8,8,128]{3,2,1,0:T(8,128)(2,1)} %bitcast.39), kind=kOutput, calls=%fused_computation.4 | convolution fusion | flops 6445596672 | bytes 13631488 | tf_op jit(solution)/shard_map/dot_general | solution.py:99
  323.7 0.0 copy-start.1
  323.7 0.0 reduce-scatter.5.cloned.1.call-update
  323.7 68.6 %reduce-scatter.5.cloned.1.call-done = bf16[128,1536]{1,0:T(8,128)(2,1)} async-done(((bf16[2048,1536]{1,0:T(8,128)(2,1)}), bf16[128,1536]{1,0:T(8,128)(2,1)}) %reduce-scatter.5.cloned.1.call-update) | async-done | bytes 393232 | tf_op jit(solution)/shard_map/reduce_scatter | solution.py:98
  392.3 1.4 reshape.125
  393.8 0.3 multiply_reduce_fusion
  394.1 0.0 copy-done.1
  394.1 0.4 fusion.19
  394.5 0.1 reshape.121
  394.6 1.0 convert_subtract_fusion
  (13 shorter events, 0.1 us)
Async XLA Ops:
  6.5 240.4 %copy-start = (bf16[128,128]{1,0:T(8,128)(2,1)S(1)}, bf16[128,128]{1,0:T(8,128)(2,1)}, u32[]{:S(2)}) copy-start(bf16[128,128]{1,0:T(8,128)(2,1)} %param.12) | copy-start | bytes 98308
  10.9 20.5 %all-to-all-start = ((s32[128,1,2]{2,1,0:T(1,128)}), s32[128,1,2]{2,1,0:T(1,128)S(1)}, u32[]{:S(2)}, u32[]{:S(2)}) async-start(s32[128,1,2]{2,1,0:T(1,128)} %bitcast.5), calls=%async_computation | async-start | bytes 131072 | tf_op jit(solution)/shard_map/all_to_all | solution.py:66
  31.3 21.0 %all-to-all-start.1 = ((bf16[128,2,1536]{2,1,0:T(2,128)(2,1)}), bf16[128,2,1536]{2,1,0:T(2,128)(2,1)S(1)}, u32[]{:S(2)}, u32[]{:S(2)}) async-start(bf16[128,2,1536]{2,1,0:T(2,128)(2,1)} %reshape.112), calls=%async_computation.1 | async-start | bytes 1572864 | tf_op jit(solution)/shard_map/all_to_all | solution.py:59
  57.7 5.0 %copy-start.2 = (s32[96,2]{0,1:T(2,128)S(1)}, s32[96,2]{0,1:T(2,128)}, u32[]{:S(2)}) copy-start(s32[96,2]{0,1:T(2,128)} %param.10) | copy-start | bytes 2308
  57.7 92.7 %all-to-all-start.2 = ((bf16[16,128,1536]{2,1,0:T(8,128)(2,1)}), bf16[16,128,1536]{2,1,0:T(8,128)(2,1)}, u32[]{:S(2)}, u32[]{:S(2)}) async-start(bf16[16,128,1536]{2,1,0:T(8,128)(2,1)} %stack.2), calls=%async_computation.2 | async-start | bytes 12582912 | tf_op jit(solution)/shard_map/all_to_all | solution.py:87
  62.5 182.7 %reduce-scatter.3.cloned.1.call-start = ((), (), s32[]{:S(2)}) async-start(), calls=%async_computation.5 | async-start | bytes 3538944 | tf_op jit(solution)/shard_map/reduce_scatter | solution.py:93
  162.0 150.4 %all-gather.2.cloned.1.call-start = ((), (), s32[]{:S(2)}) async-start(), calls=%async_computation.6 | async-start | bytes 3538944 | tf_op jit(solution)/shard_map/all_gather | solution.py:96
  250.6 141.7 %reduce-scatter.5.cloned.1.call-start = ((), (), s32[]{:S(2)}) async-start(), calls=%async_computation.7 | async-start | bytes 6684672 | tf_op jit(solution)/shard_map/reduce_scatter | solution.py:98
  323.7 70.4 %copy-start.1 = (bf16[128,128]{1,0:T(8,128)(2,1)S(1)}, bf16[128,128]{1,0:T(8,128)(2,1)}, u32[]{:S(2)}) copy-start(bf16[128,128]{1,0:T(8,128)(2,1)} %param.13) | copy-start | bytes 98308
Sparse Core Ops, SparseCore 0:
  162.1 83.0 reduce-scatter.2
  250.7 61.6 all-gather.1
  323.8 68.4 reduce-scatter.4
